TPU v7x, 128 devices: a whole 4x4x4 slice. The times are simulated.
128 devices in a mesh: dp: 16 (over y, x), expert: 8 (over z, core).
Axes of the slice: x: 4, y: 4, z: 4, core: 2. Of those that a mesh axis runs over, the one named last changes fastest.
Arguments:
- tokens: bfloat16 [4096, 4096], P('dp', 'expert'), may hold values from -100 to 100
- w_gate: bfloat16 [8, 4096, 14336], P('expert', None, 'dp'), may hold values from -0.09375 to 0.09375
- w_up: bfloat16 [8, 4096, 14336], P('expert', None, 'dp'), may hold values from -0.09375 to 0.09375
- w_down: bfloat16 [8, 14336, 4096], P('expert', 'dp'), may hold values from -0.046875 to 0.046875
- pick_block: int32 [8, 8], replicated, may hold values from 0 to 3
- pick_live: int32 [8, 8], replicated, may hold values from 0 to 1, as said below
- combine_weight: float32 [8, 8], replicated, may hold values from 0.25 to 1
Outputs:
- combined: bfloat16 [4096, 4096], P('dp', 'expert')
Inputs may be any that keep to these rules, and one draw needn't show every extreme that they name: `pick_live`: each expert takes at least one block, and some expert takes a block from every pair of dp rows.
All inputs are finite; a program needn't handle non-finite values.
Results may differ from a plain program's by a relative error of at most 0.02.
Values may be sent and summed in bfloat16 or wider, within the bound.
A program may use at most 128 MiB of HBM per device.

v0:
```python
import jax
import jax.numpy as jnp
from jax import lax
from jax.sharding import PartitionSpec as P

BLOCK = 128


def from_partner(value, axis, stride):
    return lax.ppermute(value, axis, [(i, i ^ 1 << stride) for i in range(lax.axis_size(axis))])


def rms_normalize(values, square_sums, model_width):
    values_f32 = values.astype(jnp.float32)
    inv_rms = lax.rsqrt(square_sums / model_width + 1e-05)
    return (values_f32 * inv_rms[:, None]).astype(jnp.bfloat16)


def on_device(tokens, w_gate, w_up, w_down, pick_block, pick_live, combine_weight):
    expert_count = lax.axis_size("expert")
    features_dev = tokens.shape[1]
    model_width = features_dev * expert_count
    blocks_here = tokens.shape[0] // BLOCK
    half_rows = BLOCK // 2
    row_index = lax.axis_index("dp")
    half_bit = row_index % 2
    pair_index = row_index // 2
    tokens_f32 = tokens.astype(jnp.float32)
    square_sums = lax.psum(jnp.sum(tokens_f32 * tokens_f32, axis=1), "expert")
    source = rms_normalize(tokens, square_sums, model_width)
    picked = lax.dynamic_index_in_dim(pick_block, pair_index, axis=1, keepdims=False)
    live_flags = lax.dynamic_index_in_dim(pick_live, pair_index, axis=1, keepdims=False)
    weights_here = lax.dynamic_index_in_dim(combine_weight, pair_index, axis=1, keepdims=False)
    owned_here = (live_flags == 1) & (picked // blocks_here == half_bit)
    local_block = picked % blocks_here
    blocks = source.reshape(blocks_here, BLOCK, features_dev)
    chosen = jnp.take(blocks, local_block, axis=0)
    chosen = jnp.where(owned_here[:, None, None], chosen, jnp.zeros((), jnp.bfloat16))
    arrived = lax.all_to_all(chosen, "expert", split_axis=0, concat_axis=2, tiled=True)[0]
    outgoing = lax.dynamic_slice_in_dim(arrived, (1 - half_bit) * half_rows, half_rows, 0)
    partner = from_partner(outgoing, "dp", 0)
    own_half = lax.dynamic_slice_in_dim(arrived, half_bit * half_rows, half_rows, 0)
    merged = own_half + partner
    gate_weights = w_gate[0]
    up_weights = w_up[0]
    down_weights = w_down[0]
    rows_piece = lax.all_gather(merged, "dp", axis=0, tiled=True)
    gate_proj = jnp.dot(rows_piece, gate_weights, preferred_element_type=jnp.float32)
    up_proj = jnp.dot(rows_piece, up_weights, preferred_element_type=jnp.float32)
    hidden = (jax.nn.silu(gate_proj) * up_proj).astype(jnp.bfloat16)
    partial_value = jnp.dot(hidden, down_weights, preferred_element_type=jnp.float32).astype(
        jnp.bfloat16
    )
    summed = lax.psum_scatter(
        lax.optimization_barrier(partial_value).astype(jnp.float32).astype(jnp.bfloat16),
        "dp",
        scatter_dimension=0,
        tiled=True,
    )
    spread = lax.all_to_all(summed[:, None, :], "expert", split_axis=2, concat_axis=1, tiled=True)
    other_half = from_partner(spread, "dp", 0)
    assembled = jnp.where(
        half_bit == 0,
        jnp.concatenate([spread, other_half], axis=0),
        jnp.concatenate([other_half, spread], axis=0),
    )
    slot_match = local_block[None, :] == jnp.arange(blocks_here, dtype=jnp.int32)[:, None]
    combine_coef = jnp.where(
        slot_match & owned_here[None, :], weights_here[None, :], jnp.zeros((), jnp.float32)
    )
    combined = jnp.einsum("le,red->lrd", combine_coef, assembled.astype(jnp.float32))
    return combined.astype(jnp.bfloat16).reshape(blocks_here * BLOCK, features_dev)


def solution(mesh):
    in_specs = (
        P("dp", "expert"),
        P("expert", None, "dp"),
        P("expert", None, "dp"),
        P("expert", "dp", None),
        P(),
        P(),
        P(),
    )
    out_specs = P("dp", "expert")
    return jax.shard_map(
        on_device, mesh=mesh, in_specs=in_specs, out_specs=out_specs, check_vma=False
    )
```

profile of v0, /device:TPU:0, one launch (start us, length us, event | category | flops | bytes accessed | tf_op | source)
XLA Modules:
  0.0 329.2 jit_solution(12364163355996505817)
XLA Ops:
  6.5 0.9 dynamic-slice_reduce_fusion.1
  7.5 1.1 fusion.12
  8.6 16.0 %psum.7 = f32[256]{0:T(256)S(1)} all-reduce(f32[256]{0:T(256)S(1)} %fusion.12), channel_id=1, replica_groups=mesh['dp'=16,'expert'=8] {'expert'}, use_global_device_ids=true, to_apply=%region_1.2 | all-reduce | flops 256 | bytes 2048 | tf_op jit(solution)/shard_map/psum | solution.py:29
  24.5 1.1 fusion.13
  25.6 0.9 fusion.15
  26.5 0.6 gather_fusion
  27.2 1.2 select_select_fusion
  28.4 3.6 %all-to-all-start = ((bf16[8,128,512]{2,1,0:T(8,128)(2,1)}), bf16[8,128,512]{2,1,0:T(8,128)(2,1)S(1)}, u32[]{:S(2)}, u32[]{:S(2)}) async-start(bf16[8,128,512]{2,1,0:T(8,128)(2,1)} %select_select_fusion), calls=%async_computation | async-start | bytes 2097152 | tf_op jit(solution)/shard_map/all_to_all | solution.py:39
  32.0 15.8 %all-to-all-done = bf16[8,128,512]{2,1,0:T(8,128)(2,1)S(1)} async-done(((bf16[8,128,512]{2,1,0:T(8,128)(2,1)}), bf16[8,128,512]{2,1,0:T(8,128)(2,1)S(1)}, u32[]{:S(2)}, u32[]{:S(2)}) %all-to-all-start) | async-done | bytes 1048608 | tf_op jit(solution)/shard_map/all_to_all | solution.py:39
  47.8 0.7 copy.27
  48.5 0.6 constant_dynamic-slice_fusion
  49.1 0.4 copy.29
  49.5 1.6 collective-permute-start
  51.0 0.4 copy.33
  51.4 11.6 %collective-permute-done = bf16[64,4096]{1,0:T(8,128)(2,1)S(1)} collective-permute-done((bf16[64,4096]{1,0:T(8,128)(2,1)S(1)}, bf16[64,4096]{1,0:T(8,128)(2,1)S(1)}, u32[]{:S(2)}, u32[]{:S(2)}) %collective-permute-start) | collective-permute-done | bytes 524320 | tf_op jit(solution)/shard_map/ppermute | solution.py:10
  63.0 1.0 add.73
  64.2 70.0 %all-gather.2.cloned.1.call-done = bf16[1024,4096]{1,0:T(8,128)(2,1)} async-done(((bf16[64,4096]{1,0:T(8,128)(2,1)}), bf16[1024,4096]{1,0:T(8,128)(2,1)}) %all-gather.2.cloned.1.call-update) | async-done | bytes 8388624 | tf_op jit(solution)/shard_map/all_gather | solution.py:47
  134.3 12.5 %fusion.1 = f32[1024,896]{1,0:T(8,128)S(1)} fusion(bf16[1024,4096]{1,0:T(8,128)(2,1)} %all-gather.2.cloned.1.call-done, bf16[1,4096,896]{2,1,0:T(8,128)(2,1)} %param.9), kind=kOutput, calls=%fused_computation.3 | convolution fusion | flops 7516192768 | bytes 19398656 | tf_op jit(solution)/shard_map/dot_general | solution.py:49
  146.8 15.1 %fusion.3 = f32[1024,896]{1,0:T(8,128)S(1)} fusion(bf16[1024,4096]{1,0:T(8,128)(2,1)S(1)} %copy-done.1, bf16[1,4096,896]{2,1,0:T(8,128)(2,1)} %param.8), kind=kOutput, calls=%fused_computation.5 | convolution fusion | flops 7516192768 | bytes 19398656 | tf_op jit(solution)/shard_map/dot_general | solution.py:48
  161.9 14.1 %convolution_convert_fusion = bf16[1024,4096]{1,0:T(8,128)(2,1)} fusion(bf16[1,896,4096]{2,1,0:T(8,128)(2,1)} %param.10, f32[1024,896]{1,0:T(8,128)S(1)} %fusion.1, f32[1024,896]{1,0:T(8,128)S(1)} %fusion.3), kind=kOutput, calls=%fused_computation.1 | convolution fusion | flops 7525892096 | bytes 23068672 | tf_op jit(solution)/shard_map/dot_general | solution.py:51
  176.0 84.8 %reduce-scatter.2.cloned.1.call-done = bf16[64,4096]{1,0:T(8,128)(2,1)} async-done(((bf16[1024,4096]{1,0:T(8,128)(2,1)}), bf16[64,4096]{1,0:T(8,128)(2,1)}) %reduce-scatter.2.cloned.1.call-update) | async-done | bytes 524304 | tf_op jit(solution)/shard_map/reduce_scatter | solution.py:54
  260.7 4.9 %copy.30 = bf16[64,1,4096]{0,1,2:T(2,128)(2,1)S(1)} copy(bf16[64,1,4096]{2,0,1:T(8,128)(2,1)} %bitcast.33) | data formatting | bytes 1048576 | tf_op jit(solution)/shard_map/broadcast_in_dim | solution.py:60
  265.6 0.5 broadcast.170
  266.1 22.6 %reduce.10 = bf16[4096,64]{1,0:T(8,128)(2,1)S(1)} reduce(bf16[4096,1,64]{2,1,0:T(2,128)(2,1)S(1)} %bitcast.29, bf16[]{:T(256)} %broadcast.170), dimensions={1}, to_apply=%bitcast.23.reduce_sub_computation | reduce | bytes 1048578
  288.8 0.7 reshape.126
  289.5 14.6 %all_to_all.27 = bf16[8,2,16384]{2,1,0:T(2,128)(2,1)S(1)} all-to-all(bf16[8,2,16384]{2,1,0:T(2,128)(2,1)S(1)} %reshape.126), channel_id=1, replica_groups=mesh['dp'=16,'expert'=8] {'expert'}, dimensions={0} | all-to-all | bytes 1048576 | tf_op jit(solution)/shard_map/all_to_all | solution.py:60
  304.1 1.2 reshape.127
  305.4 2.3 copy.31
  307.8 1.5 collective-permute-start.1
  309.5 11.7 %collective-permute-done.1 = bf16[64,8,512]{2,1,0:T(8,128)(2,1)S(1)} collective-permute-done((bf16[64,8,512]{2,1,0:T(8,128)(2,1)S(1)}, bf16[64,8,512]{2,1,0:T(8,128)(2,1)S(1)}, u32[]{:S(2)}, u32[]{:S(2)}) %collective-permute-start.1) | collective-permute-done | bytes 524320 | tf_op jit(solution)/shard_map/ppermute | solution.py:10
  321.2 0.4 convolution_convert_fusion.1
  321.6 0.7 copy.32
  (14 shorter events, 0.7 us)
Async XLA Ops:
  6.5 302.8 %copy-start = (f32[8,8]{1,0:T(8,128)S(1)}, f32[8,8]{1,0:T(8,128)}, u32[]{:S(2)}) copy-start(f32[8,8]{1,0:T(8,128)} %param.13) | copy-start | bytes 772
  28.4 19.4 %all-to-all-start = ((bf16[8,128,512]{2,1,0:T(8,128)(2,1)}), bf16[8,128,512]{2,1,0:T(8,128)(2,1)S(1)}, u32[]{:S(2)}, u32[]{:S(2)}) async-start(bf16[8,128,512]{2,1,0:T(8,128)(2,1)} %select_select_fusion), calls=%async_computation | async-start | bytes 2097152 | tf_op jit(solution)/shard_map/all_to_all | solution.py:39
  31.9 102.4 %all-gather.2.cloned.1.call-start = ((), (), s32[]{:S(2)}) async-start(), calls=%async_computation.3 | async-start | bytes 8912896 | tf_op jit(solution)/shard_map/all_gather | solution.py:47
  49.5 13.5 %collective-permute-start = (bf16[64,4096]{1,0:T(8,128)(2,1)S(1)}, bf16[64,4096]{1,0:T(8,128)(2,1)S(1)}, u32[]{:S(2)}, u32[]{:S(2)}) collective-permute-start(bf16[64,4096]{1,0:T(8,128)(2,1)S(1)} %copy.29), channel_id=1, source_target_pairs={{0,8},{8,0},{16,24},{24,16},{32,40},{40,32},{48,56},{56,48},{64,72... | collective-permute-start | bytes 1572872 | tf_op jit(solution)/shard_map/ppermute | solution.py:10
  64.0 196.7 %reduce-scatter.2.cloned.1.call-start = ((), (), s32[]{:S(2)}) async-start(), calls=%async_computation.4 | async-start | bytes 8912896 | tf_op jit(solution)/shard_map/reduce_scatter | solution.py:54
  134.3 12.5 %copy-start.1 = (bf16[1024,4096]{1,0:T(8,128)(2,1)S(1)}, bf16[1024,4096]{1,0:T(8,128)(2,1)}, u32[]{:S(2)}) copy-start(bf16[1024,4096]{1,0:T(8,128)(2,1)} %all-gather.2.cloned.1.call-done) | copy-start | bytes 25165828
  307.8 13.4 %collective-permute-start.1 = (bf16[64,8,512]{2,1,0:T(8,128)(2,1)S(1)}, bf16[64,8,512]{2,1,0:T(8,128)(2,1)S(1)}, u32[]{:S(2)}, u32[]{:S(2)}) collective-permute-start(bf16[64,8,512]{2,1,0:T(8,128)(2,1)S(1)} %bitcast.34), channel_id=1, source_target_pairs={{0,8},{8,0},{16,24},{24,16},{32,40},{40,32},{48,56},{56,48},{64,72... | collective-permute-start | bytes 1572872 | tf_op jit(solution)/shard_map/ppermute | solution.py:10
Sparse Core Ops, SparseCore 0:
  64.1 70.0 all-gather.1
  176.1 84.5 reduce-scatter.1
where the time goes:
time: 330 us; the launch traced here: 329 us
  waiting for transfers between devices  194 us (59%)
  matrix products  42.1 us (13%)
  blocking collectives  30.6 us (9%)
  other arithmetic  28.8 us (9%)
  between operations  13.6 us (4%)
  local copies, waits for them, and re-layouts  13.3 us (4%)
  starting transfers between devices  6.86 us (2%)
    reduce_scatter x1, waiting for transfers between devices, on_device(): lax.psum_scatter(lax.optimization_barrier(partial_value).astype(jnp.float...  84.8 us
    all_gather x1, waiting for transfers between devices, on_device(): rows_piece = lax.all_gather(merged, 'dp', axis=0, tiled=True)  70 us
    ppermute x2, waiting for transfers between devices, from_partner(): lax.ppermute(value, axis, [(i, i ^ 1 << stride) for i in range(lax.axis_s...  23.3 us
    unnamed x1, other arithmetic  22.6 us
    psum x1, blocking collectives, on_device(): square_sums = lax.psum(jnp.sum(tokens_f32 * tokens_f32, axis=1), 'expert')  16 us
    all_to_all x1, waiting for transfers between devices, on_device(): lax.all_to_all(chosen, 'expert', split_axis=0, concat_axis=2, tiled=True)[0]  15.8 us
    dot_general x1, matrix products, on_device(): jnp.dot(rows_piece, gate_weights, preferred_element_type=jnp.float32)  15.1 us
    all_to_all x1, blocking collectives, on_device(): lax.all_to_all(summed[:, None, :], 'expert', split_axis=2, concat_axis=1,...  14.6 us
  transfers between devices with their start and end apart: 5, of which 5 were waited for; matrix products, arithmetic and copies ran while one was open for 0% of the time, Pallas kernels for 0%

commit v1 on v0

--- a/solution.py
+++ b/solution.py
@@ -57,7 +57,19 @@
         scatter_dimension=0,
         tiled=True,
     )
-    spread = lax.all_to_all(summed[:, None, :], "expert", split_axis=2, concat_axis=1, tiled=True)
+    x = summed[:, None, :]
+    ways, here = (lax.axis_size("expert"), lax.axis_index("expert"))
+    width = x.shape[2] // ways
+    shape = list(x.shape)
+    shape[2] = width
+    height = shape[1]
+    shape[1] = height * ways
+    spread = jnp.zeros(shape, x.dtype)
+    for mask in range(ways):
+        part = lax.dynamic_slice_in_dim(x, (here ^ mask) * width, width, axis=2)
+        if mask:
+            part = lax.ppermute(part, "expert", [(d, d ^ mask) for d in range(ways)])
+        spread = lax.dynamic_update_slice_in_dim(spread, part, (here ^ mask) * height, axis=1)
     other_half = from_partner(spread, "dp", 0)
     assembled = jnp.where(
         half_bit == 0,

time: 330 us -> 301 us (0.912)
  other arithmetic: 28.8 us -> 6.14 us
  blocking collectives: 30.6 us -> 16 us
  starting transfers between devices: 6.86 us -> 15.1 us
    unnamed x1, other arithmetic: 22.6 us -> 0.01 us
    all_to_all x1 -> x0, blocking collectives: 14.6 us -> none  [on_device(): lax.all_to_all(summed[:, None, :], 'expert', split_axis=2, concat_axis=1,...]
    dynamic_update_slice x0 -> x8, local copies, waits for them, and re-layouts: none -> 9.33 us  [on_device(): lax.dynamic_update_slice_in_dim(spread, part, (here ^ mask) * height, axi...]
    ppermute x0 -> x7, starting transfers between devices: none -> 8.22 us  [on_device(): part = lax.ppermute(part, 'expert', [(d, d ^ mask) for d in range(ways)])]
    broadcast_in_dim x1, local copies, waits for them, and re-layouts: 4.86 us -> 0.04 us  [on_device(): spread = jnp.zeros(shape, x.dtype)]
  transfers between devices with their start and end apart: 5 -> 12, of which waited for: 5 -> 5; matrix products, arithmetic and copies ran while one was open for 0% -> 3% of each run, Pallas kernels for 0% -> 0%
where the time goes in v1:
time: 301 us; the launch traced here: 300 us
  waiting for transfers between devices  195 us (65%)
  matrix products  39.4 us (13%)
  blocking collectives  16 us (5%)
  starting transfers between devices  15.1 us (5%)
  local copies, waits for them, and re-layouts  14.9 us (5%)
  between operations  13.8 us (5%)
  other arithmetic  6.14 us (2%)
    reduce_scatter x1, waiting for transfers between devices, on_device(): lax.psum_scatter(lax.optimization_barrier(partial_value).astype(jnp.float...  84.7 us
    all_gather x1, waiting for transfers between devices, on_device(): rows_piece = lax.all_gather(merged, 'dp', axis=0, tiled=True)  70 us
    ppermute x2, waiting for transfers between devices, from_partner(): lax.ppermute(value, axis, [(i, i ^ 1 << stride) for i in range(lax.axis_s...  24.1 us
    psum x1, blocking collectives, on_device(): square_sums = lax.psum(jnp.sum(tokens_f32 * tokens_f32, axis=1), 'expert')  16 us
    all_to_all x1, waiting for transfers between devices, on_device(): lax.all_to_all(chosen, 'expert', split_axis=0, concat_axis=2, tiled=True)[0]  15.8 us
    dot_general x1, matrix products, on_device(): jnp.dot(rows_piece, gate_weights, preferred_element_type=jnp.float32)  15.2 us
    dot_general x1, matrix products, on_device(): jnp.dot(rows_piece, up_weights, preferred_element_type=jnp.float32)  12.5 us
    dot_general x1, matrix products, on_device(): jnp.dot(hidden, down_weights, preferred_element_type=jnp.float32)  11.3 us
  transfers between devices with their start and end apart: 12, of which 5 were waited for; matrix products, arithmetic and copies ran while one was open for 3% of the time, Pallas kernels for 0%

profile of v1, /device:TPU:0, one launch (start us, length us, event | category | flops | bytes accessed | tf_op | source)
XLA Modules:
  0.0 300.0 jit_solution(6768124152524399149)
XLA Ops:
  6.5 0.9 dynamic-slice_reduce_fusion.1
  7.5 1.1 fusion.12
  8.6 16.0 %psum.7 = f32[256]{0:T(256)S(1)} all-reduce(f32[256]{0:T(256)S(1)} %fusion.12), channel_id=1, replica_groups=mesh['dp'=16,'expert'=8] {'expert'}, use_global_device_ids=true, to_apply=%region_1.2 | all-reduce | flops 256 | bytes 2048 | tf_op jit(solution)/shard_map/psum | solution.py:29
  24.5 1.1 fusion.13
  25.6 0.9 fusion.15
  27.2 1.2 select_select_fusion
  28.3 3.6 %all-to-all-start = ((bf16[8,128,512]{2,1,0:T(8,128)(2,1)}), bf16[8,128,512]{2,1,0:T(8,128)(2,1)S(1)}, u32[]{:S(2)}, u32[]{:S(2)}) async-start(bf16[8,128,512]{2,1,0:T(8,128)(2,1)} %select_select_fusion), calls=%async_computation | async-start | bytes 2097152 | tf_op jit(solution)/shard_map/all_to_all | solution.py:39
  32.0 15.8 %all-to-all-done = bf16[8,128,512]{2,1,0:T(8,128)(2,1)S(1)} async-done(((bf16[8,128,512]{2,1,0:T(8,128)(2,1)}), bf16[8,128,512]{2,1,0:T(8,128)(2,1)S(1)}, u32[]{:S(2)}, u32[]{:S(2)}) %all-to-all-start) | async-done | bytes 1048608 | tf_op jit(solution)/shard_map/all_to_all | solution.py:39
  47.8 0.7 copy.40
  49.5 1.6 collective-permute-start
  51.4 11.6 %collective-permute-done = bf16[64,4096]{1,0:T(8,128)(2,1)S(1)} collective-permute-done((bf16[64,4096]{1,0:T(8,128)(2,1)S(1)}, bf16[64,4096]{1,0:T(8,128)(2,1)S(1)}, u32[]{:S(2)}, u32[]{:S(2)}) %collective-permute-start) | collective-permute-done | bytes 524320 | tf_op jit(solution)/shard_map/ppermute | solution.py:10
  63.0 1.0 add.121
  64.2 70.0 %all-gather.2.cloned.1.call-done = bf16[1024,4096]{1,0:T(8,128)(2,1)} async-done(((bf16[64,4096]{1,0:T(8,128)(2,1)}), bf16[1024,4096]{1,0:T(8,128)(2,1)}) %all-gather.2.cloned.1.call-update) | async-done | bytes 8388624 | tf_op jit(solution)/shard_map/all_gather | solution.py:47
  134.3 12.5 %fusion.1 = f32[1024,896]{1,0:T(8,128)S(1)} fusion(bf16[1024,4096]{1,0:T(8,128)(2,1)} %all-gather.2.cloned.1.call-done, bf16[1,4096,896]{2,1,0:T(8,128)(2,1)} %param.9), kind=kOutput, calls=%fused_computation.3 | convolution fusion | flops 7516192768 | bytes 19398656 | tf_op jit(solution)/shard_map/dot_general | solution.py:49
  146.8 15.2 %fusion.3 = f32[1024,896]{1,0:T(8,128)S(1)} fusion(bf16[1024,4096]{1,0:T(8,128)(2,1)S(1)} %copy-done.1, bf16[1,4096,896]{2,1,0:T(8,128)(2,1)} %param.8), kind=kOutput, calls=%fused_computation.5 | convolution fusion | flops 7516192768 | bytes 19398656 | tf_op jit(solution)/shard_map/dot_general | solution.py:48
  162.0 11.3 %convolution_convert_fusion = bf16[1024,4096]{1,0:T(8,128)(2,1)} fusion(bf16[1,896,4096]{2,1,0:T(8,128)(2,1)S(1)} %bitcast.40, f32[1024,896]{1,0:T(8,128)S(1)} %fusion.1, f32[1024,896]{1,0:T(8,128)S(1)} %fusion.3), kind=kOutput, calls=%fused_computation.1 | convolution fusion | flops 7525892096 | bytes 23068672 | tf_op jit(solution)/shard_map/dot_general | solution.py:51
  173.4 84.7 %reduce-scatter.2.cloned.1.call-done = bf16[64,4096]{1,0:T(8,128)(2,1)} async-done(((bf16[1024,4096]{1,0:T(8,128)(2,1)}), bf16[64,4096]{1,0:T(8,128)(2,1)}) %reduce-scatter.2.cloned.1.call-update) | async-done | bytes 524304 | tf_op jit(solution)/shard_map/reduce_scatter | solution.py:54
  258.1 1.1 dynamic-slice_bitcast_fusion
  259.3 1.7 collective-permute-start.2
  261.1 3.2 %collective-permute-start.4 = (bf16[64,1,512]{2,0,1:T(8,128)(2,1)S(1)}, bf16[64,1,512]{2,0,1:T(8,128)(2,1)S(1)}, u32[]{:S(2)}, u32[]{:S(2)}) collective-permute-start(bf16[64,1,512]{2,0,1:T(8,128)(2,1)S(1)} %get-tuple-element.12), channel_id=1, source_target_pairs={{0,4},{1,5},{2,6},{3,7},{4,0},{5,1},{6,2},{7,3},{8,12},{9,13},{10,... | collective-permute-start | bytes 196616 | tf_op jit(solution)/shard_map/ppermute | solution.py:71
  264.4 2.9 collective-permute-start.6
  267.6 1.2 dynamic_update_slice.24
  268.9 1.2 dynamic_update_slice.25
  270.1 1.2 dynamic_update_slice.26
  271.4 1.2 dynamic_update_slice.27
  272.7 1.2 dynamic_update_slice.28
  274.0 1.2 dynamic_update_slice.29
  275.3 1.2 dynamic_update_slice.30
  276.6 1.2 dynamic_update_slice.31
  277.8 1.5 collective-permute-start.8
  279.5 12.5 %collective-permute-done.8 = bf16[64,8,512]{2,1,0:T(8,128)(2,1)S(1)} collective-permute-done((bf16[64,8,512]{2,1,0:T(8,128)(2,1)S(1)}, bf16[64,8,512]{2,1,0:T(8,128)(2,1)S(1)}, u32[]{:S(2)}, u32[]{:S(2)}) %collective-permute-start.8) | collective-permute-done | bytes 524320 | tf_op jit(solution)/shard_map/ppermute | solution.py:10
  292.4 0.7 copy.51
  (43 shorter events, 4.3 us)
Async XLA Ops:
  6.5 272.8 %copy-start = (f32[8,8]{1,0:T(8,128)S(1)}, f32[8,8]{1,0:T(8,128)}, u32[]{:S(2)}) copy-start(f32[8,8]{1,0:T(8,128)} %param.13) | copy-start | bytes 772
  28.3 19.4 %all-to-all-start = ((bf16[8,128,512]{2,1,0:T(8,128)(2,1)}), bf16[8,128,512]{2,1,0:T(8,128)(2,1)S(1)}, u32[]{:S(2)}, u32[]{:S(2)}) async-start(bf16[8,128,512]{2,1,0:T(8,128)(2,1)} %select_select_fusion), calls=%async_computation | async-start | bytes 2097152 | tf_op jit(solution)/shard_map/all_to_all | solution.py:39
  31.9 102.3 %all-gather.2.cloned.1.call-start = ((), (), s32[]{:S(2)}) async-start(), calls=%async_computation.2 | async-start | bytes 8912896 | tf_op jit(solution)/shard_map/all_gather | solution.py:47
  49.5 13.5 %collective-permute-start = (bf16[64,4096]{1,0:T(8,128)(2,1)S(1)}, bf16[64,4096]{1,0:T(8,128)(2,1)S(1)}, u32[]{:S(2)}, u32[]{:S(2)}) collective-permute-start(bf16[64,4096]{1,0:T(8,128)(2,1)S(1)} %copy.42), channel_id=1, source_target_pairs={{0,8},{8,0},{16,24},{24,16},{32,40},{40,32},{48,56},{56,48},{64,72... | collective-permute-start | bytes 1572872 | tf_op jit(solution)/shard_map/ppermute | solution.py:10
  64.0 194.1 %reduce-scatter.2.cloned.1.call-start = ((), (), s32[]{:S(2)}) async-start(), calls=%async_computation.3 | async-start | bytes 8912896 | tf_op jit(solution)/shard_map/reduce_scatter | solution.py:54
  134.2 12.5 %copy-start.1 = (bf16[1024,4096]{1,0:T(8,128)(2,1)S(1)}, bf16[1024,4096]{1,0:T(8,128)(2,1)}, u32[]{:S(2)}) copy-start(bf16[1024,4096]{1,0:T(8,128)(2,1)} %all-gather.2.cloned.1.call-done) | copy-start | bytes 25165828
  134.3 27.7 %slice-start = ((s8[7340032]{0:T(1024)(128)(4,1)}), s8[4194304]{0:T(1024)(128)(4,1)S(1)}, s32[]{:S(2)}) async-start(s8[7340032]{0:T(1024)(128)(4,1)} %bitcast.39), calls=%async_computation.4 | async-start | bytes 8388608
  146.8 15.2 %slice-start.1 = ((s8[7340032]{0:T(1024)(128)(4,1)}), s8[3145728]{0:T(1024)(128)(4,1)S(1)}, s32[]{:S(2)}) async-start(s8[7340032]{0:T(1024)(128)(4,1)} %bitcast.39), calls=%async_computation.5 | async-start | bytes 6291456
  259.2 5.2 %collective-permute-start.1 = (bf16[64,1,512]{2,0,1:T(8,128)(2,1)S(1)}, bf16[64,1,512]{2,0,1:T(8,128)(2,1)S(1)}, u32[]{:S(2)}, u32[]{:S(2)}) collective-permute-start(bf16[64,1,512]{2,0,1:T(8,128)(2,1)S(1)} %get-tuple-element.15), channel_id=1, source_target_pairs={{0,1},{1,0},{2,3},{3,2},{4,5},{5,4},{6,7},{7,6},{8,9},{9,8},{10,11... | collective-permute-start | bytes 196616 | tf_op jit(solution)/shard_map/ppermute | solution.py:71
  259.3 8.0 %collective-permute-start.2 = (bf16[64,1,512]{2,0,1:T(8,128)(2,1)S(1)}, bf16[64,1,512]{2,0,1:T(8,128)(2,1)S(1)}, u32[]{:S(2)}, u32[]{:S(2)}) collective-permute-start(bf16[64,1,512]{2,0,1:T(8,128)(2,1)S(1)} %get-tuple-element.14), channel_id=1, source_target_pairs={{0,2},{1,3},{2,0},{3,1},{4,6},{5,7},{6,4},{7,5},{8,10},{9,11},{10,... | collective-permute-start | bytes 196616 | tf_op jit(solution)/shard_map/ppermute | solution.py:71
  260.9 10.4 %collective-permute-start.3 = (bf16[64,1,512]{2,0,1:T(8,128)(2,1)S(1)}, bf16[64,1,512]{2,0,1:T(8,128)(2,1)S(1)}, u32[]{:S(2)}, u32[]{:S(2)}) collective-permute-start(bf16[64,1,512]{2,0,1:T(8,128)(2,1)S(1)} %get-tuple-element.13), channel_id=1, source_target_pairs={{0,3},{1,2},{2,1},{3,0},{4,7},{5,6},{6,5},{7,4},{8,11},{9,10},{10,... | collective-permute-start | bytes 196616 | tf_op jit(solution)/shard_map/ppermute | solution.py:71
  261.1 11.5 %collective-permute-start.4 = (bf16[64,1,512]{2,0,1:T(8,128)(2,1)S(1)}, bf16[64,1,512]{2,0,1:T(8,128)(2,1)S(1)}, u32[]{:S(2)}, u32[]{:S(2)}) collective-permute-start(bf16[64,1,512]{2,0,1:T(8,128)(2,1)S(1)} %get-tuple-element.12), channel_id=1, source_target_pairs={{0,4},{1,5},{2,6},{3,7},{4,0},{5,1},{6,2},{7,3},{8,12},{9,13},{10,... | collective-permute-start | bytes 196616 | tf_op jit(solution)/shard_map/ppermute | solution.py:71
  264.3 9.6 %collective-permute-start.5 = (bf16[64,1,512]{2,0,1:T(8,128)(2,1)S(1)}, bf16[64,1,512]{2,0,1:T(8,128)(2,1)S(1)}, u32[]{:S(2)}, u32[]{:S(2)}) collective-permute-start(bf16[64,1,512]{2,0,1:T(8,128)(2,1)S(1)} %get-tuple-element.11), channel_id=1, source_target_pairs={{0,5},{1,4},{2,7},{3,6},{4,1},{5,0},{6,3},{7,2},{8,13},{9,12},{10,... | collective-permute-start | bytes 196616 | tf_op jit(solution)/shard_map/ppermute | solution.py:71
  264.4 10.8 %collective-permute-start.6 = (bf16[64,1,512]{2,0,1:T(8,128)(2,1)S(1)}, bf16[64,1,512]{2,0,1:T(8,128)(2,1)S(1)}, u32[]{:S(2)}, u32[]{:S(2)}) collective-permute-start(bf16[64,1,512]{2,0,1:T(8,128)(2,1)S(1)} %get-tuple-element.10), channel_id=1, source_target_pairs={{0,6},{1,7},{2,4},{3,5},{4,2},{5,3},{6,0},{7,1},{8,14},{9,15},{10,... | collective-permute-start | bytes 196616 | tf_op jit(solution)/shard_map/ppermute | solution.py:71
  267.3 9.2 %collective-permute-start.7 = (bf16[64,1,512]{2,0,1:T(8,128)(2,1)S(1)}, bf16[64,1,512]{2,0,1:T(8,128)(2,1)S(1)}, u32[]{:S(2)}, u32[]{:S(2)}) collective-permute-start(bf16[64,1,512]{2,0,1:T(8,128)(2,1)S(1)} %get-tuple-element.9), channel_id=1, source_target_pairs={{0,7},{1,6},{2,5},{3,4},{4,3},{5,2},{6,1},{7,0},{8,15},{9,14},{10,... | collective-permute-start | bytes 196616 | tf_op jit(solution)/shard_map/ppermute | solution.py:71
  277.8 14.2 %collective-permute-start.8 = (bf16[64,8,512]{2,1,0:T(8,128)(2,1)S(1)}, bf16[64,8,512]{2,1,0:T(8,128)(2,1)S(1)}, u32[]{:S(2)}, u32[]{:S(2)}) collective-permute-start(bf16[64,8,512]{2,1,0:T(8,128)(2,1)S(1)} %dynamic_update_slice.31), channel_id=1, source_target_pairs={{0,8},{8,0},{16,24},{24,16},{32,40},{40,32},{48,56},{56,48},{64,72... | collective-permute-start | bytes 1572872 | tf_op jit(solution)/shard_map/ppermute | solution.py:10
Sparse Core Ops, SparseCore 0:
  64.1 70.0 all-gather.1
  173.5 84.5 reduce-scatter.1
